TPU v7x, 128 devices: a whole 4x4x4 slice. The times are simulated.
128 devices in a mesh: section: 2 (over z_lo), dp: 8 (over z_hi, y), ctx: 8 (over x, core).
Axes of the slice: x: 4, y: 4, z: 4 (z_hi: 2, z_lo: 2; z = z_hi * 2 + z_lo), core: 2. Of those that a mesh axis runs over, the one named last changes fastest.
Arguments:
- token_ids: int32 [2048], P('ctx'), may hold values from 0 to 511
- embedding: bfloat16 [512, 4096], P(None, 'dp'), may hold values from -6 to 6
- project_in: bfloat16 [2, 4096, 3, 4096], P('section', 'ctx', None, 'dp'), may hold values from -0.09375 to 0.09375
- short_taps: float32 [2, 3, 3, 4096], P('section', None, None, 'dp'), may hold values from -3.5 to 3.5
- filter_taps: float32 [2, 128, 4096], P('section', None, 'dp'), may hold values from -0.5 to 0.5
- decay_rates: float32 [2, 4096], P('section', 'dp'), may hold values from 0.5 to 4
- project_out: bfloat16 [2, 4096, 4096], P('section', 'dp', 'ctx'), may hold values from -0.09375 to 0.09375
- cotangent: bfloat16 [2048, 4096], P('ctx', 'dp'), may hold values from -0.125 to 0.125
Outputs:
- grad_project_in: float32 [2, 4096, 3, 4096], P('section', 'ctx', None, 'dp')
- grad_project_out: float32 [2, 4096, 4096], P('section', 'dp', 'ctx')
- grad_filter: float32 [2, 128, 4096], P('section', None, 'dp')
- grad_decay: float32 [2, 4096], P('section', 'dp')
- grad_short: float32 [2, 3, 3, 4096], P('section', None, None, 'dp')
All inputs are finite; a program needn't handle non-finite values.
Results may differ from a plain program's by a relative error of at most 0.03.
Values may be sent and summed in bfloat16 or wider, within the bound.
A program may use at most 128 MiB of HBM per device.

v0:
```python
import jax
import jax.numpy as jnp
from jax import lax
from jax.sharding import PartitionSpec as P

EPSILON = 1e-06


def gather_turned(arrays, axis, dims):
    turned = [jnp.moveaxis(a, dim, 0) for a, dim in zip(arrays, dims)]
    both = jnp.concatenate([t.reshape(len(t), -1) for t in turned], axis=1)
    filled, at, finished = (lax.all_gather(both, axis, axis=0, tiled=True), 0, [])
    for t, dim in zip(turned, dims):
        section = filled[:, at : at + t[0].size].reshape(-1, *t.shape[1:])
        finished.append(jnp.moveaxis(section, 0, dim))
        at += t[0].size
    return tuple(finished)


def laid_out(pieces, dim):
    pieces = jnp.moveaxis(pieces, 0, dim)
    shape = pieces.shape
    return pieces.reshape(*shape[:dim], shape[dim] * shape[dim + 1], *shape[dim + 2 :])


def from_everyone(shard, axis):
    copies = jnp.broadcast_to(shard, (lax.axis_size(axis), *shard.shape))
    return lax.all_to_all(copies, axis, split_axis=0, concat_axis=0, tiled=True)


def gather_directly(shard, axis, dim):
    return laid_out(from_everyone(shard, axis), dim)


def from_behind(value, axis, steps):
    count = lax.axis_size(axis)
    initial, last = (max(0, -steps), min(count, count - steps))
    return lax.ppermute(value, axis, [(source, source + steps) for source in range(initial, last)])


def cut_along(shard, dim, peers):
    shape = shard.shape
    pieces = shard.reshape(*shape[:dim], peers, shape[dim] // peers, *shape[dim + 1 :])
    return jnp.moveaxis(pieces, dim, 0)


def summed_on_arrival(shard, axis, dim):
    peers = lax.axis_size(axis)
    pieces = lax.all_to_all(cut_along(shard, dim, peers), axis, 0, 0, tiled=True)
    return jnp.sum(pieces.astype(jnp.float32), axis=0)


def taken_together(shard, axis):
    everything = from_everyone(shard, axis)
    return jnp.sum(everything, axis=0)


def over_copies(shard, axis):
    everything = from_everyone(shard, axis)
    return jnp.sum(everything.astype(jnp.float32), axis=0)


def correlate(signal, kernel):
    channels = signal.shape[1]
    result = lax.conv_general_dilated(
        signal[None],
        kernel[:, None, :],
        (1,),
        "VALID",
        dimension_numbers=("NWC", "WIO", "NWC"),
        feature_group_count=channels,
        precision=lax.Precision.HIGHEST,
    )
    return result[0]


def local(
    token_ids, embedding, project_in, short_taps, filter_taps, decay_rates, project_out, cotangent
):
    section_zero = lax.axis_index("section") == 0
    tok_rows = token_ids.shape[0]
    weights_in, weights_out = gather_turned((project_in[0], project_out[0]), "ctx", (0, 1))
    full_width = weights_in.shape[0]
    chan_count = weights_in.shape[2]
    flat_in = weights_in.reshape(full_width, 3 * chan_count)
    taps_local = short_taps[0]
    filter_local = filter_taps[0]
    tap_count = filter_local.shape[0]
    positions = jnp.arange(tap_count).astype(jnp.float32)
    damping = jnp.exp(-decay_rates[0][None, :] * positions[:, None] / tap_count)
    kernel = filter_local * damping
    onehot = (
        token_ids[:, None] == jnp.arange(embedding.shape[0], dtype=jnp.int32)[None, :]
    ).astype(jnp.bfloat16)
    first_input = jnp.dot(onehot, embedding, preferred_element_type=jnp.float32).astype(
        jnp.bfloat16
    )

    def forward(inputs, apply_out):
        rows_all = gather_directly(inputs, "dp", 1)
        rows_float = rows_all.astype(jnp.float32)
        inv_rms = lax.rsqrt(jnp.mean(rows_float * rows_float, axis=1, keepdims=True) + EPSILON)
        normed = (rows_float * inv_rms).astype(jnp.bfloat16)
        projected = jnp.dot(normed, flat_in, preferred_element_type=jnp.float32).reshape(
            tok_rows, 3, chan_count
        )
        earlier = from_behind(projected[tok_rows - 2 :], "ctx", 1)
        padded_proj = jnp.concatenate([earlier, projected], axis=0)
        shortened = (
            taps_local[0] * padded_proj[2:]
            + taps_local[1] * padded_proj[1:-1]
            + taps_local[2] * padded_proj[:-2]
        )
        products = shortened[:, 1] * shortened[:, 2]
        earlier_prod = from_behind(
            products[tok_rows - tap_count + 1 :].astype(jnp.bfloat16), "ctx", 1
        ).astype(jnp.float32)
        padded_prod = jnp.concatenate([earlier_prod, products], axis=0)
        filtered = correlate(padded_prod, kernel[::-1])
        gated_rows = (shortened[:, 0] * filtered).astype(jnp.bfloat16)
        saved = (
            inputs,
            rows_float,
            inv_rms,
            normed,
            padded_proj,
            shortened,
            padded_prod,
            filtered,
            gated_rows,
        )
        if apply_out:
            partials = jnp.dot(gated_rows, weights_out, preferred_element_type=jnp.float32)
            summed = summed_on_arrival(partials.astype(jnp.bfloat16), "dp", 1)
            return ((inputs.astype(jnp.float32) + summed).astype(jnp.bfloat16), saved)
        return (None, saved)

    def backward(saved, grad_local, need_input):
        (
            inputs,
            rows_float,
            inv_rms,
            normed,
            padded_proj,
            shortened,
            padded_prod,
            filtered,
            gated_rows,
        ) = saved
        grad_rows = gather_directly(grad_local, "dp", 1)
        grad_gated = lax.dot_general(
            grad_rows, weights_out, (((1,), (1,)), ((), ())), preferred_element_type=jnp.float32
        )
        grad_query = grad_gated * filtered
        grad_filtered = grad_gated * shortened[:, 0]
        later_rows = from_behind(
            grad_filtered[: tap_count - 1].astype(jnp.bfloat16), "ctx", -1
        ).astype(jnp.float32)
        grad_prod = correlate(jnp.concatenate([grad_filtered, later_rows], axis=0), kernel)
        grad_kernel = correlate(padded_prod, grad_filtered)[::-1]
        grad_short_out = jnp.stack(
            [grad_query, grad_prod * shortened[:, 2], grad_prod * shortened[:, 1]], axis=1
        )
        later_short = from_behind(grad_short_out[:2], "ctx", -1)
        padded_short = jnp.concatenate([grad_short_out, later_short], axis=0)
        grad_proj = (
            taps_local[0] * padded_short[:-2]
            + taps_local[1] * padded_short[1:-1]
            + taps_local[2] * padded_short[2:]
        )
        grad_taps = jnp.stack(
            [
                jnp.sum(grad_short_out * padded_proj[2:], axis=0),
                jnp.sum(grad_short_out * padded_proj[1:-1], axis=0),
                jnp.sum(grad_short_out * padded_proj[:-2], axis=0),
            ],
            axis=0,
        )
        grad_proj_b = grad_proj.astype(jnp.bfloat16)
        grad_inputs = None
        if need_input:
            partials = lax.dot_general(
                grad_proj_b.reshape(tok_rows, 3 * chan_count),
                flat_in,
                (((1,), (1,)), ((), ())),
                preferred_element_type=jnp.float32,
            )
            shared_part = summed_on_arrival(partials.astype(jnp.bfloat16), "dp", 1)
            own_rows = inputs.astype(jnp.float32)
            row_stat = (
                taken_together(jnp.sum(own_rows * shared_part, axis=1), "dp")[:, None] / full_width
            )
            local_grad = inv_rms * shared_part - own_rows * inv_rms**3 * row_stat
            grad_inputs = (grad_local.astype(jnp.float32) + local_grad).astype(jnp.bfloat16)
        return (grad_inputs, (normed, gated_rows, grad_rows, grad_proj_b, grad_kernel, grad_taps))

    out_first, saved_first = forward(first_input, True)
    arrived = from_behind(out_first, "section", 1)
    unused_out, saved_second = forward(arrived, False)
    back_grad, late_parts = backward(saved_second, cotangent, True)
    returned = from_behind(back_grad, "section", -1)
    unused_grad, early_parts = backward(saved_first, returned, False)
    normed, gated_rows, grad_rows, grad_proj_b, grad_kernel, grad_taps = tuple(
        (
            jnp.where(section_zero, early_item, late_item)
            for early_item, late_item in zip(early_parts, late_parts)
        )
    )
    kernel_sum, taps_sum = (
        over_copies(grad_kernel.astype(jnp.bfloat16), "ctx").astype(jnp.float32),
        over_copies(grad_taps.astype(jnp.bfloat16), "ctx").astype(jnp.float32),
    )
    grad_filter = kernel_sum * damping
    grad_decay = (
        -jnp.sum(kernel_sum * filter_local * damping * positions[:, None], axis=0) / tap_count
    )
    flat_grad = grad_proj_b.reshape(tok_rows, 3 * chan_count)
    row_block = lax.slice_in_dim(
        normed, 0, full_width // lax.axis_size("ctx") * lax.axis_size("ctx"), axis=1
    )
    grad_in = lax.psum_scatter(
        lax.dot_general(
            row_block, flat_grad, (((0,), (0,)), ((), ())), preferred_element_type=jnp.float32
        )
        .reshape(full_width // lax.axis_size("ctx") * lax.axis_size("ctx"), 3, chan_count)
        .astype(jnp.bfloat16),
        "ctx",
        scatter_dimension=0,
        tiled=True,
    ).astype(jnp.float32)
    out_partials = lax.dot_general(
        gated_rows, grad_rows, (((0,), (0,)), ((), ())), preferred_element_type=jnp.float32
    )
    grad_out = summed_on_arrival(out_partials.astype(jnp.bfloat16), "ctx", 1)
    return (grad_in[None], grad_out[None], grad_filter[None], grad_decay[None], taps_sum[None])


def solution(mesh):
    return jax.shard_map(
        local,
        mesh=mesh,
        in_specs=(
            P("ctx"),
            P(None, "dp"),
            P("section", "ctx", None, "dp"),
            P("section", None, None, "dp"),
            P("section", None, "dp"),
            P("section", "dp"),
            P("section", "dp", "ctx"),
            P("ctx", "dp"),
        ),
        out_specs=(
            P("section", "ctx", None, "dp"),
            P("section", "dp", "ctx"),
            P("section", None, "dp"),
            P("section", "dp"),
            P("section", None, None, "dp"),
        ),
        check_vma=False,
    )
```

profile of v0, /device:TPU:1, one launch (start us, length us, event | category | flops | bytes accessed | tf_op | source)
XLA Modules:
  0.0 550.6 jit_solution(13177721387538396610)
XLA Ops:
  13.2 8.5 %all-to-all-start = ((bf16[8,256,512]{1,2,0:T(8,128)(2,1)}), bf16[8,256,512]{1,2,0:T(8,128)(2,1)S(1)}, u32[]{:S(2)}, u32[]{:S(2)}) async-start(bf16[8,256,512]{1,2,0:T(8,128)(2,1)} %broadcast_in_dim.68), calls=%async_computation | async-start | bytes 4194304 | tf_op jit(solution)/shard_map/all_to_all | solution.py:28
  21.9 28.4 %all-to-all-done = bf16[8,256,512]{1,2,0:T(8,128)(2,1)S(1)} async-done(((bf16[8,256,512]{1,2,0:T(8,128)(2,1)}), bf16[8,256,512]{1,2,0:T(8,128)(2,1)S(1)}, u32[]{:S(2)}, u32[]{:S(2)}) %all-to-all-start) | async-done | bytes 2097184 | tf_op jit(solution)/shard_map/all_to_all | solution.py:28
  52.7 46.5 %all-gather.2.cloned.1.call-done = bf16[4096,2048]{0,1:T(8,128)(2,1)} async-done(((bf16[512,2048]{0,1:T(8,128)(2,1)}), bf16[4096,2048]{0,1:T(8,128)(2,1)}) %all-gather.2.cloned.1.call-update) | async-done | bytes 16777232 | tf_op jit(solution)/shard_map/all_gather | solution.py:12
  99.2 7.1 %fusion.4 = f32[256,1536]{1,0:T(8,128)S(1)} fusion(bf16[256,4096]{0,1:T(8,128)(2,1)} %fusion.10, bf16[4096,2048]{0,1:T(8,128)(2,1)} %all-gather.2.cloned.1.call-done), kind=kOutput, calls=%fused_computation.4 | convolution fusion | flops 3221225472 | bytes 16252928 | tf_op jit(solution)/shard_map/dot_general | solution.py:104
  125.7 5.3 fusion.64
  134.9 35.3 %all_to_all.51 = bf16[8,256,512]{2,1,0:T(8,128)(2,1)S(1)} all-to-all(bf16[8,256,512]{2,1,0:T(8,128)(2,1)S(1)} %bitcast.181), channel_id=1, replica_groups=mesh['section'=2,'dp'=8,'ctx'=8] {'dp'}, dimensions={0} | all-to-all | bytes 4194304 | tf_op jit(solution)/shard_map/all_to_all | solution.py:49
  172.9 5.2 collective-permute-done.2
  184.4 28.5 %all-to-all-done.2 = bf16[8,256,512]{1,2,0:T(8,128)(2,1)} async-done(((bf16[8,256,512]{1,2,0:T(8,128)(2,1)}), bf16[8,256,512]{1,2,0:T(8,128)(2,1)}, u32[]{:S(2)}, u32[]{:S(2)}) %all-to-all-start.2) | async-done | bytes 2097184 | tf_op jit(solution)/shard_map/all_to_all | solution.py:28
  223.4 6.5 %fusion.2 = f32[256,1536]{1,0:T(8,128)S(1)} fusion(bf16[256,4096]{0,1:T(8,128)(2,1)S(1)} %fusion.9, bf16[4096,2048]{0,1:T(8,128)(2,1)} %all-gather.2.cloned.1.call-done), kind=kOutput, calls=%fused_computation.2 | convolution fusion | flops 3221225472 | bytes 16252928 | tf_op jit(solution)/shard_map/dot_general | solution.py:104
  257.9 5.3 fusion.32
  267.4 5.3 fusion.49
  282.0 8.3 %fusion.6 = bf16[256,4096]{1,0:T(8,128)(2,1)S(1)} fusion(bf16[256,1536]{0,1:T(8,128)(2,1)} %bitcast.195, bf16[4096,2048]{0,1:T(8,128)(2,1)} %all-gather.2.cloned.1.call-done), kind=kOutput, calls=%fused_computation.9 | convolution fusion | flops 3222274048 | bytes 15466496 | tf_op jit(solution)/shard_map/dot_general | solution.py:182
  290.5 30.1 %all_to_all.52 = bf16[8,256,512]{2,1,0:T(8,128)(2,1)S(1)} all-to-all(bf16[8,256,512]{2,1,0:T(8,128)(2,1)S(1)} %bitcast.182), channel_id=1, replica_groups=mesh['section'=2,'dp'=8,'ctx'=8] {'dp'}, dimensions={0} | all-to-all | bytes 4194304 | tf_op jit(solution)/shard_map/all_to_all | solution.py:49
  321.7 8.9 %all_to_all.53 = f32[8,1,256]{2,1,0:T(1,128)S(1)} all-to-all(f32[8,1,256]{2,1,0:T(1,128)S(1)} %broadcast_in_dim.75), channel_id=1, replica_groups=mesh['section'=2,'dp'=8,'ctx'=8] {'dp'}, dimensions={0} | all-to-all | bytes 16384 | tf_op jit(solution)/shard_map/all_to_all | solution.py:28
  333.2 8.4 %collective-permute-done.7 = bf16[256,512]{1,0:T(8,128)(2,1)S(1)} collective-permute-done((bf16[256,512]{1,0:T(8,128)(2,1)S(1)}, bf16[256,512]{1,0:T(8,128)(2,1)S(1)}, u32[]{:S(2)}, u32[]{:S(2)}) %collective-permute-start.7) | collective-permute-done | bytes 262176 | tf_op jit(solution)/shard_map/ppermute | solution.py:38
  341.9 30.2 %all_to_all.54 = bf16[8,256,512]{1,2,0:T(8,128)(2,1)S(1)} all-to-all(bf16[8,256,512]{1,2,0:T(8,128)(2,1)S(1)} %broadcast_in_dim.76), channel_id=1, replica_groups=mesh['section'=2,'dp'=8,'ctx'=8] {'dp'}, dimensions={0} | all-to-all | bytes 4194304 | tf_op jit(solution)/shard_map/all_to_all | solution.py:28
  386.6 5.3 fusion.30
  404.0 8.0 %convolution_convert_fusion = bf16[4096,3,512]{2,0,1:T(8,128)(2,1)} fusion(bf16[256,4096,1]{0,1,2:T(8,128)(2,1)} %bitcast.183, bf16[256,3,512]{0,2,1:T(8,128)(2,1)S(1)} %copy.184), kind=kOutput, calls=%fused_computation.6 | convolution fusion | flops 3227516928 | bytes 15466496 | tf_op jit(solution)/shard_map/dot_general | solution.py:222
  415.0 5.3 fusion.44
  425.6 5.3 fusion.46
  441.7 5.6 %all-to-all-done.9 = bf16[8,3,3,512]{3,2,1,0:T(4,128)(2,1)S(1)} async-done(((bf16[8,3,3,512]{3,2,1,0:T(4,128)(2,1)}), bf16[8,3,3,512]{3,2,1,0:T(4,128)(2,1)S(1)}, u32[]{:S(2)}, u32[]{:S(2)}) %all-to-all-start.9) | async-done | bytes 73760 | tf_op jit(solution)/shard_map/all_to_all | solution.py:28
  460.2 13.5 %all-to-all-done.8 = bf16[8,128,512]{2,1,0:T(8,128)(2,1)S(1)} async-done(((bf16[8,128,512]{2,1,0:T(8,128)(2,1)}), bf16[8,128,512]{2,1,0:T(8,128)(2,1)S(1)}, u32[]{:S(2)}, u32[]{:S(2)}) %all-to-all-start.8) | async-done | bytes 1048608 | tf_op jit(solution)/shard_map/all_to_all | solution.py:28
  473.8 5.5 all-to-all-start.7
  481.8 54.3 %all-to-all-done.7 = bf16[8,512,512]{2,1,0:T(8,128)(2,1)} async-done(((bf16[8,512,512]{2,1,0:T(8,128)(2,1)}), bf16[8,512,512]{2,1,0:T(8,128)(2,1)}, u32[]{:S(2)}, u32[]{:S(2)}) %all-to-all-start.7) | async-done | bytes 4194336 | tf_op jit(solution)/shard_map/all_to_all | solution.py:49
  (222 shorter events, 164.6 us)
Async XLA Ops:
  7.2 92.0 %all-gather.2.cloned.1.call-start = ((), (), s32[]{:S(2)}) async-start(), calls=%async_computation.11 | async-start | bytes 18874368 | tf_op jit(solution)/shard_map/all_gather | solution.py:12
  13.2 8.5 %copy-start.20 = (f32[1,128,512]{2,1,0:T(8,128)S(1)}, f32[1,128,512]{2,1,0:T(8,128)}, u32[]{:S(2)}) copy-start(f32[1,128,512]{2,1,0:T(8,128)} %param.12) | copy-start | bytes 786436
  13.2 37.1 %all-to-all-start = ((bf16[8,256,512]{1,2,0:T(8,128)(2,1)}), bf16[8,256,512]{1,2,0:T(8,128)(2,1)S(1)}, u32[]{:S(2)}, u32[]{:S(2)}) async-start(bf16[8,256,512]{1,2,0:T(8,128)(2,1)} %broadcast_in_dim.68), calls=%async_computation | async-start | bytes 4194304 | tf_op jit(solution)/shard_map/all_to_all | solution.py:28
  21.7 232.5 %copy-start.39 = (f32[1,512]{1,0:T(1,128)}, f32[1,512]{1,0:T(1,128)S(1)}, u32[]{:S(2)}) copy-start(f32[1,512]{1,0:T(1,128)S(1)} %neg.14) | copy-start | bytes 6148
  21.7 232.5 %copy-start.42 = (f32[128]{0:T(128)}, f32[128]{0:T(128)S(1)}, u32[]{:S(2)}) copy-start(f32[128]{0:T(128)S(1)} %iota_convert_fusion) | copy-start | bytes 1540
  107.5 9.1 %collective-permute-start = (f32[2,3,512]{2,0,1:T(2,128)S(1)}, f32[2,3,512]{2,0,1:T(2,128)S(1)}, u32[]{:S(2)}, u32[]{:S(2)}) collective-permute-start(f32[2,3,512]{2,0,1:T(2,128)S(1)} %bitcast.214), channel_id=1, source_target_pairs={{0,1},{1,2},{2,3},{3,4},{4,5},{5,6},{6,7},{8,9},{9,10},{10,11},{11... | collective-permute-start | bytes 36872 | tf_op jit(solution)/shard_map/ppermute | solution.py:38
  119.9 11.1 %copy-start.2 = (f32[256,3,512]{2,0,1:T(8,128)}, f32[256,3,512]{2,0,1:T(8,128)S(1)}, u32[]{:S(2)}) copy-start(f32[256,3,512]{2,0,1:T(8,128)S(1)} %multiply_add_fusion.1) | copy-start | bytes 4718596
  120.1 4.1 collective-permute-start.1
  170.6 7.5 %collective-permute-start.2 = (bf16[256,512]{1,0:T(8,128)(2,1)S(1)}, bf16[256,512]{1,0:T(8,128)(2,1)S(1)}, u32[]{:S(2)}, u32[]{:S(2)}) collective-permute-start(bf16[256,512]{1,0:T(8,128)(2,1)S(1)} %add_convert_fusion), channel_id=1, source_target_pairs={{0,64},{1,65},{2,66},{3,67},{4,68},{5,69},{6,70},{7,71},{8,72},{9,... | collective-permute-start | bytes 786440 | tf_op jit(solution)/shard_map/ppermute | solution.py:38
  179.7 33.1 %all-to-all-start.2 = ((bf16[8,256,512]{1,2,0:T(8,128)(2,1)}), bf16[8,256,512]{1,2,0:T(8,128)(2,1)}, u32[]{:S(2)}, u32[]{:S(2)}) async-start(bf16[8,256,512]{1,2,0:T(8,128)(2,1)} %broadcast_in_dim.71), calls=%async_computation.2 | async-start | bytes 4194304 | tf_op jit(solution)/shard_map/all_to_all | solution.py:28
  214.3 33.0 %all-to-all-start.3 = ((bf16[8,256,512]{1,2,0:T(8,128)(2,1)}), bf16[8,256,512]{1,2,0:T(8,128)(2,1)}, u32[]{:S(2)}, u32[]{:S(2)}) async-start(bf16[8,256,512]{1,2,0:T(8,128)(2,1)} %broadcast_in_dim.72), calls=%async_computation.3 | async-start | bytes 4194304 | tf_op jit(solution)/shard_map/all_to_all | solution.py:28
  218.7 321.3 %reduce-scatter.2.cloned.1.call-start = ((), (), s32[]{:S(2)}) async-start(), calls=%async_computation.12 | async-start | bytes 14155776 | tf_op jit(solution)/shard_map/reduce_scatter | solution.py:221
  231.1 8.0 %collective-permute-start.3 = (f32[2,3,512]{2,0,1:T(2,128)S(1)}, f32[2,3,512]{2,0,1:T(2,128)S(1)}, u32[]{:S(2)}, u32[]{:S(2)}) collective-permute-start(f32[2,3,512]{2,0,1:T(2,128)S(1)} %bitcast.215), channel_id=1, source_target_pairs={{0,1},{1,2},{2,3},{3,4},{4,5},{5,6},{6,7},{8,9},{9,10},{10,11},{11... | collective-permute-start | bytes 36872 | tf_op jit(solution)/shard_map/ppermute | solution.py:38
  251.5 11.8 %copy-start.28 = (f32[256,512]{1,0:T(8,128)}, f32[256,512]{1,0:T(8,128)S(1)}, u32[]{:S(2)}) copy-start(f32[256,512]{1,0:T(8,128)S(1)} %get-tuple-element.38) | copy-start | bytes 1572868
  251.5 6.3 %collective-permute-start.5 = (bf16[127,512]{1,0:T(8,128)(2,1)S(1)}, bf16[127,512]{1,0:T(8,128)(2,1)S(1)}, u32[]{:S(2)}, u32[]{:S(2)}) collective-permute-start(bf16[127,512]{1,0:T(8,128)(2,1)S(1)} %slice.267), channel_id=1, source_target_pairs={{1,0},{2,1},{3,2},{4,3},{5,4},{6,5},{7,6},{9,8},{10,9},{11,10},{12... | collective-permute-start | bytes 390152 | tf_op jit(solution)/shard_map/ppermute | solution.py:38
  263.4 3.9 collective-permute-start.4
  273.7 6.0 %collective-permute-start.6 = (f32[2,3,512]{2,0,1:T(2,128)S(1)}, f32[2,3,512]{2,0,1:T(2,128)S(1)}, u32[]{:S(2)}, u32[]{:S(2)}) collective-permute-start(f32[2,3,512]{2,0,1:T(2,128)S(1)} %slice.161), channel_id=1, source_target_pairs={{1,0},{2,1},{3,2},{4,3},{5,4},{6,5},{7,6},{9,8},{10,9},{11,10},{12... | collective-permute-start | bytes 36872 | tf_op jit(solution)/shard_map/ppermute | solution.py:38
  331.9 9.7 %collective-permute-start.7 = (bf16[256,512]{1,0:T(8,128)(2,1)S(1)}, bf16[256,512]{1,0:T(8,128)(2,1)S(1)}, u32[]{:S(2)}, u32[]{:S(2)}) collective-permute-start(bf16[256,512]{1,0:T(8,128)(2,1)S(1)} %fusion.37), channel_id=1, source_target_pairs={{64,0},{65,1},{66,2},{67,3},{68,4},{69,5},{70,6},{71,7},{72,8},{73... | collective-permute-start | bytes 786440 | tf_op jit(solution)/shard_map/ppermute | solution.py:38
  341.9 30.2 %copy-start.25 = (f32[1,256,512]{2,0,1:T(1,128)S(1)}, f32[1,256,512]{2,0,1:T(1,128)}, u32[]{:S(2)}) copy-start(f32[1,256,512]{2,0,1:T(1,128)} %copy-done.24) | copy-start | bytes 1572868
  378.0 6.6 %collective-permute-start.8 = (bf16[127,512]{1,0:T(8,128)(2,1)}, bf16[127,512]{1,0:T(8,128)(2,1)}, u32[]{:S(2)}, u32[]{:S(2)}) collective-permute-start(bf16[127,512]{1,0:T(8,128)(2,1)} %slice.266), channel_id=1, source_target_pairs={{1,0},{2,1},{3,2},{4,3},{5,4},{6,5},{7,6},{9,8},{10,9},{11,10},{12... | collective-permute-start | bytes 390152 | tf_op jit(solution)/shard_map/ppermute | solution.py:38
  395.1 5.8 %collective-permute-start.9 = (f32[2,3,512]{2,0,1:T(2,128)S(1)}, f32[2,3,512]{2,0,1:T(2,128)S(1)}, u32[]{:S(2)}, u32[]{:S(2)}) collective-permute-start(f32[2,3,512]{2,0,1:T(2,128)S(1)} %slice.165), channel_id=1, source_target_pairs={{1,0},{2,1},{3,2},{4,3},{5,4},{6,5},{7,6},{9,8},{10,9},{11,10},{12... | collective-permute-start | bytes 36872 | tf_op jit(solution)/shard_map/ppermute | solution.py:38
  438.2 9.1 %all-to-all-start.9 = ((bf16[8,3,3,512]{3,2,1,0:T(4,128)(2,1)}), bf16[8,3,3,512]{3,2,1,0:T(4,128)(2,1)S(1)}, u32[]{:S(2)}, u32[]{:S(2)}) async-start(bf16[8,3,3,512]{3,2,1,0:T(4,128)(2,1)} %broadcast_in_dim.84), calls=%async_computation.10 | async-start | bytes 196608 | tf_op jit(solution)/shard_map/all_to_all | solution.py:28
  448.3 25.4 %all-to-all-start.8 = ((bf16[8,128,512]{2,1,0:T(8,128)(2,1)}), bf16[8,128,512]{2,1,0:T(8,128)(2,1)S(1)}, u32[]{:S(2)}, u32[]{:S(2)}) async-start(bf16[8,128,512]{2,1,0:T(8,128)(2,1)} %broadcast_in_dim.83), calls=%async_computation.9 | async-start | bytes 2097152 | tf_op jit(solution)/shard_map/all_to_all | solution.py:28
  473.8 62.3 %all-to-all-start.7 = ((bf16[8,512,512]{2,1,0:T(8,128)(2,1)}), bf16[8,512,512]{2,1,0:T(8,128)(2,1)}, u32[]{:S(2)}, u32[]{:S(2)}) async-start(bf16[8,512,512]{2,1,0:T(8,128)(2,1)} %bitcast.178), calls=%async_computation.8 | async-start | bytes 8388608 | tf_op jit(solution)/shard_map/all_to_all | solution.py:49
  (40 other events, 132.6 us)
Sparse Core Ops, SparseCore 0:
  10.7 88.4 all-gather.1
  412.1 95.6 reduce-scatter.1
where the time goes:
time: 560 us; the launch traced here: 551 us
  waiting for transfers between devices  208 us (37%)
  blocking collectives  105 us (19%)
  matrix products  75.8 us (14%)
  starting transfers between devices  54.7 us (10%)
  local copies, waits for them, and re-layouts  49.2 us (9%)
  other arithmetic  43.2 us (8%)
  between operations  15.2 us (3%)
    all_to_all x5, waiting for transfers between devices, from_everyone(): return lax.all_to_all(copies, axis, split_axis=0, concat_axis=0, tiled=True)  79.9 us
    all_to_all x2, blocking collectives, summed_on_arrival(): lax.all_to_all(cut_along(shard, dim, peers), axis, 0, 0, tiled=True)  65.4 us
    all_to_all x1, waiting for transfers between devices, summed_on_arrival(): lax.all_to_all(cut_along(shard, dim, peers), axis, 0, 0, tiled=True)  54.3 us
    all_gather x1, waiting for transfers between devices, gather_turned(): lax.all_gather(both, axis, axis=0, tiled=True)  46.5 us
    all_to_all x2, blocking collectives, from_everyone(): return lax.all_to_all(copies, axis, split_axis=0, concat_axis=0, tiled=True)  39.1 us
    conv_general_dilated x6, matrix products, correlate(): lax.conv_general_dilated(signal[None], kernel[:, None, :], (1,), 'VALID',...  31.8 us
    ppermute x10, waiting for transfers between devices, from_behind(): lax.ppermute(value, axis, [(source, source + steps) for source in range(i...  27 us
    all_to_all x5, starting transfers between devices, from_everyone(): return lax.all_to_all(copies, axis, split_axis=0, concat_axis=0, tiled=True)  25.1 us
  transfers between devices with their start and end apart: 18, of which 14 were waited for; matrix products, arithmetic and copies ran while one was open for 13% of the time, Pallas kernels for 0%

commit v1 on v0

--- a/solution.py
+++ b/solution.py
@@ -9,7 +9,13 @@
 def gather_turned(arrays, axis, dims):
     turned = [jnp.moveaxis(a, dim, 0) for a, dim in zip(arrays, dims)]
     both = jnp.concatenate([t.reshape(len(t), -1) for t in turned], axis=1)
-    filled, at, finished = (lax.all_gather(both, axis, axis=0, tiled=True), 0, [])
+    filled, at, finished = (
+        jnp.concatenate(
+            lax.all_to_all(jnp.stack([both] * lax.axis_size(axis)), axis, 0, 0), axis=0
+        ),
+        0,
+        [],
+    )
     for t, dim in zip(turned, dims):
         section = filled[:, at : at + t[0].size].reshape(-1, *t.shape[1:])
         finished.append(jnp.moveaxis(section, 0, dim))

time: 560 us -> 708 us (1.26)
  waiting for transfers between devices: 208 us -> 333 us
  local copies, waits for them, and re-layouts: 49.2 us -> 61.4 us
  starting transfers between devices: 54.7 us -> 61.9 us
    all_to_all x0 -> x1, waiting for transfers between devices: none -> 181 us  [gather_turned(): lax.all_to_all(jnp.stack([both] * lax.axis_size(axis)), axis, 0, 0)]
    all_gather x1 -> x0, waiting for transfers between devices: 46.5 us -> none  [gather_turned(): lax.all_gather(both, axis, axis=0, tiled=True)]
    all_to_all x5, waiting for transfers between devices: 79.9 us -> 70.8 us  [from_everyone(): return lax.all_to_all(copies, axis, split_axis=0, concat_axis=0, tiled=True)]
    unnamed x99 -> x97, local copies, waits for them, and re-layouts: 13.8 us -> 15 us
  transfers between devices with their start and end apart: 18 -> 18, of which waited for: 14 -> 14; matrix products, arithmetic and copies ran while one was open for 13% -> 12% of each run, Pallas kernels for 0% -> 0%
where the time goes in v1:
time: 708 us; the launch traced here: 698 us
  waiting for transfers between devices  333 us (47%)
  blocking collectives  106 us (15%)
  matrix products  76.4 us (11%)
  starting transfers between devices  61.9 us (9%)
  local copies, waits for them, and re-layouts  61.4 us (9%)
  other arithmetic  44.4 us (6%)
  between operations  15.2 us (2%)
    all_to_all x1, waiting for transfers between devices, gather_turned(): lax.all_to_all(jnp.stack([both] * lax.axis_size(axis)), axis, 0, 0)  181 us
    all_to_all x5, waiting for transfers between devices, from_everyone(): return lax.all_to_all(copies, axis, split_axis=0, concat_axis=0, tiled=True)  70.8 us
    all_to_all x2, blocking collectives, summed_on_arrival(): lax.all_to_all(cut_along(shard, dim, peers), axis, 0, 0, tiled=True)  66.4 us
    all_to_all x1, waiting for transfers between devices, summed_on_arrival(): lax.all_to_all(cut_along(shard, dim, peers), axis, 0, 0, tiled=True)  54.3 us
    all_to_all x2, blocking collectives, from_everyone(): return lax.all_to_all(copies, axis, split_axis=0, concat_axis=0, tiled=True)  39.1 us
    conv_general_dilated x6, matrix products, correlate(): lax.conv_general_dilated(signal[None], kernel[:, None, :], (1,), 'VALID',...  31.8 us
    ppermute x10, waiting for transfers between devices, from_behind(): lax.ppermute(value, axis, [(source, source + steps) for source in range(i...  26.8 us
    all_to_all x5, starting transfers between devices, from_everyone(): return lax.all_to_all(copies, axis, split_axis=0, concat_axis=0, tiled=True)  25.5 us
  transfers between devices with their start and end apart: 18, of which 14 were waited for; matrix products, arithmetic and copies ran while one was open for 12% of the time, Pallas kernels for 0%

profile of v1, /device:TPU:1, one launch (start us, length us, event | category | flops | bytes accessed | tf_op | source)
XLA Modules:
  0.0 697.9 jit_solution(632705426574937655)
XLA Ops:
  10.9 8.3 %all-to-all-start = ((bf16[8,256,512]{1,2,0:T(8,128)(2,1)}), bf16[8,256,512]{1,2,0:T(8,128)(2,1)S(1)}, u32[]{:S(2)}, u32[]{:S(2)}) async-start(bf16[8,256,512]{1,2,0:T(8,128)(2,1)} %broadcast_in_dim.68), calls=%async_computation | async-start | bytes 4194304 | tf_op jit(solution)/shard_map/all_to_all | solution.py:34
  28.7 19.1 %all-to-all-done = bf16[8,256,512]{1,2,0:T(8,128)(2,1)S(1)} async-done(((bf16[8,256,512]{1,2,0:T(8,128)(2,1)}), bf16[8,256,512]{1,2,0:T(8,128)(2,1)S(1)}, u32[]{:S(2)}, u32[]{:S(2)}) %all-to-all-start) | async-done | bytes 2097184 | tf_op jit(solution)/shard_map/all_to_all | solution.py:34
  47.8 7.0 stack.55
  54.8 6.6 all-to-all-start.1
  63.9 181.1 %all-to-all-done.1 = bf16[8,512,2048]{2,1,0:T(8,128)(2,1)} async-done(((bf16[8,512,2048]{2,1,0:T(8,128)(2,1)}), bf16[8,512,2048]{2,1,0:T(8,128)(2,1)}, u32[]{:S(2)}, u32[]{:S(2)}) %all-to-all-start.1) | async-done | bytes 16777248 | tf_op jit(solution)/shard_map/all_to_all | solution.py:14
  245.0 7.1 %fusion.4 = f32[256,1536]{1,0:T(8,128)S(1)} fusion(bf16[256,4096]{0,1:T(8,128)(2,1)} %fusion.10, bf16[4096,2048]{1,0:T(8,128)(2,1)} %bitcast.5), kind=kOutput, calls=%fused_computation.4 | convolution fusion | flops 3221225472 | bytes 16252928 | tf_op jit(solution)/shard_map/dot_general | solution.py:110
  271.4 5.3 fusion.64
  280.6 34.3 %all_to_all.56 = bf16[8,256,512]{2,1,0:T(8,128)(2,1)S(1)} all-to-all(bf16[8,256,512]{2,1,0:T(8,128)(2,1)S(1)} %bitcast.182), channel_id=1, replica_groups=mesh['section'=2,'dp'=8,'ctx'=8] {'dp'}, dimensions={0} | all-to-all | bytes 4194304 | tf_op jit(solution)/shard_map/all_to_all | solution.py:55
  329.2 28.5 %all-to-all-done.3 = bf16[8,256,512]{1,2,0:T(8,128)(2,1)} async-done(((bf16[8,256,512]{1,2,0:T(8,128)(2,1)}), bf16[8,256,512]{1,2,0:T(8,128)(2,1)}, u32[]{:S(2)}, u32[]{:S(2)}) %all-to-all-start.3) | async-done | bytes 2097184 | tf_op jit(solution)/shard_map/all_to_all | solution.py:34
  368.2 6.5 fusion.2
  402.8 5.3 fusion.32
  412.3 5.3 fusion.49
  426.9 8.3 %fusion.6 = bf16[256,4096]{1,0:T(8,128)(2,1)S(1)} fusion(bf16[256,1536]{0,1:T(8,128)(2,1)} %bitcast.196, bf16[4096,2048]{1,0:T(8,128)(2,1)} %bitcast.5), kind=kOutput, calls=%fused_computation.9 | convolution fusion | flops 3222274048 | bytes 15466496 | tf_op jit(solution)/shard_map/dot_general | solution.py:188
  435.4 32.2 %all_to_all.57 = bf16[8,256,512]{2,1,0:T(8,128)(2,1)S(1)} all-to-all(bf16[8,256,512]{2,1,0:T(8,128)(2,1)S(1)} %bitcast.183), channel_id=1, replica_groups=mesh['section'=2,'dp'=8,'ctx'=8] {'dp'}, dimensions={0} | all-to-all | bytes 4194304 | tf_op jit(solution)/shard_map/all_to_all | solution.py:55
  468.7 8.9 %all_to_all.58 = f32[8,1,256]{2,1,0:T(1,128)S(1)} all-to-all(f32[8,1,256]{2,1,0:T(1,128)S(1)} %broadcast_in_dim.75), channel_id=1, replica_groups=mesh['section'=2,'dp'=8,'ctx'=8] {'dp'}, dimensions={0} | all-to-all | bytes 16384 | tf_op jit(solution)/shard_map/all_to_all | solution.py:34
  480.2 8.4 %collective-permute-done.7 = bf16[256,512]{1,0:T(8,128)(2,1)S(1)} collective-permute-done((bf16[256,512]{1,0:T(8,128)(2,1)S(1)}, bf16[256,512]{1,0:T(8,128)(2,1)S(1)}, u32[]{:S(2)}, u32[]{:S(2)}) %collective-permute-start.7) | collective-permute-done | bytes 262176 | tf_op jit(solution)/shard_map/ppermute | solution.py:44
  488.8 30.2 %all_to_all.59 = bf16[8,256,512]{1,2,0:T(8,128)(2,1)S(1)} all-to-all(bf16[8,256,512]{1,2,0:T(8,128)(2,1)S(1)} %broadcast_in_dim.76), channel_id=1, replica_groups=mesh['section'=2,'dp'=8,'ctx'=8] {'dp'}, dimensions={0} | all-to-all | bytes 4194304 | tf_op jit(solution)/shard_map/all_to_all | solution.py:34
  533.5 5.3 fusion.30
  550.9 8.0 %convolution_convert_fusion = bf16[4096,3,512]{2,0,1:T(8,128)(2,1)} fusion(bf16[256,4096,1]{0,1,2:T(8,128)(2,1)} %bitcast.184, bf16[256,3,512]{0,2,1:T(8,128)(2,1)S(1)} %copy.189), kind=kOutput, calls=%fused_computation.6 | convolution fusion | flops 3227516928 | bytes 15466496 | tf_op jit(solution)/shard_map/dot_general | solution.py:228
  562.0 5.3 fusion.44
  589.0 5.6 all-to-all-done.10
  607.6 13.6 %all-to-all-done.9 = bf16[8,128,512]{2,1,0:T(8,128)(2,1)S(1)} async-done(((bf16[8,128,512]{2,1,0:T(8,128)(2,1)}), bf16[8,128,512]{2,1,0:T(8,128)(2,1)S(1)}, u32[]{:S(2)}, u32[]{:S(2)}) %all-to-all-start.9) | async-done | bytes 1048608 | tf_op jit(solution)/shard_map/all_to_all | solution.py:34
  621.1 5.5 all-to-all-start.8
  629.2 54.3 %all-to-all-done.8 = bf16[8,512,512]{2,1,0:T(8,128)(2,1)} async-done(((bf16[8,512,512]{2,1,0:T(8,128)(2,1)}), bf16[8,512,512]{2,1,0:T(8,128)(2,1)}, u32[]{:S(2)}, u32[]{:S(2)}) %all-to-all-start.8) | async-done | bytes 4194336 | tf_op jit(solution)/shard_map/all_to_all | solution.py:55
  (221 shorter events, 182.8 us)
Async XLA Ops:
  10.9 36.9 %all-to-all-start = ((bf16[8,256,512]{1,2,0:T(8,128)(2,1)}), bf16[8,256,512]{1,2,0:T(8,128)(2,1)S(1)}, u32[]{:S(2)}, u32[]{:S(2)}) async-start(bf16[8,256,512]{1,2,0:T(8,128)(2,1)} %broadcast_in_dim.68), calls=%async_computation | async-start | bytes 4194304 | tf_op jit(solution)/shard_map/all_to_all | solution.py:34
  54.8 190.2 %all-to-all-start.1 = ((bf16[8,512,2048]{2,1,0:T(8,128)(2,1)}), bf16[8,512,2048]{2,1,0:T(8,128)(2,1)}, u32[]{:S(2)}, u32[]{:S(2)}) async-start(bf16[8,512,2048]{2,1,0:T(8,128)(2,1)} %stack.55), calls=%async_computation.1 | async-start | bytes 33554432 | tf_op jit(solution)/shard_map/all_to_all | solution.py:14
  61.3 337.7 %copy-start.39 = (f32[1,512]{1,0:T(1,128)}, f32[1,512]{1,0:T(1,128)S(1)}, u32[]{:S(2)}) copy-start(f32[1,512]{1,0:T(1,128)S(1)} %neg.14) | copy-start | bytes 6148
  61.4 337.7 %copy-start.42 = (f32[128]{0:T(128)}, f32[128]{0:T(128)S(1)}, u32[]{:S(2)}) copy-start(f32[128]{0:T(128)S(1)} %iota_convert_fusion) | copy-start | bytes 1540
  253.3 9.3 %collective-permute-start = (f32[2,3,512]{2,0,1:T(2,128)S(1)}, f32[2,3,512]{2,0,1:T(2,128)S(1)}, u32[]{:S(2)}, u32[]{:S(2)}) collective-permute-start(f32[2,3,512]{2,0,1:T(2,128)S(1)} %bitcast.215), channel_id=1, source_target_pairs={{0,1},{1,2},{2,3},{3,4},{4,5},{5,6},{6,7},{8,9},{9,10},{10,11},{11... | collective-permute-start | bytes 36872 | tf_op jit(solution)/shard_map/ppermute | solution.py:44
  265.9 10.8 %copy-start.2 = (f32[256,3,512]{2,0,1:T(8,128)}, f32[256,3,512]{2,0,1:T(8,128)S(1)}, u32[]{:S(2)}) copy-start(f32[256,3,512]{2,0,1:T(8,128)S(1)} %multiply_add_fusion.1) | copy-start | bytes 4718596
  266.0 3.9 collective-permute-start.1
  315.3 7.6 %collective-permute-start.2 = (bf16[256,512]{1,0:T(8,128)(2,1)S(1)}, bf16[256,512]{1,0:T(8,128)(2,1)S(1)}, u32[]{:S(2)}, u32[]{:S(2)}) collective-permute-start(bf16[256,512]{1,0:T(8,128)(2,1)S(1)} %add_convert_fusion), channel_id=1, source_target_pairs={{0,64},{1,65},{2,66},{3,67},{4,68},{5,69},{6,70},{7,71},{8,72},{9,... | collective-permute-start | bytes 786440 | tf_op jit(solution)/shard_map/ppermute | solution.py:44
  324.5 33.1 %all-to-all-start.3 = ((bf16[8,256,512]{1,2,0:T(8,128)(2,1)}), bf16[8,256,512]{1,2,0:T(8,128)(2,1)}, u32[]{:S(2)}, u32[]{:S(2)}) async-start(bf16[8,256,512]{1,2,0:T(8,128)(2,1)} %broadcast_in_dim.71), calls=%async_computation.3 | async-start | bytes 4194304 | tf_op jit(solution)/shard_map/all_to_all | solution.py:34
  359.1 33.0 %all-to-all-start.4 = ((bf16[8,256,512]{1,2,0:T(8,128)(2,1)}), bf16[8,256,512]{1,2,0:T(8,128)(2,1)}, u32[]{:S(2)}, u32[]{:S(2)}) async-start(bf16[8,256,512]{1,2,0:T(8,128)(2,1)} %broadcast_in_dim.72), calls=%async_computation.4 | async-start | bytes 4194304 | tf_op jit(solution)/shard_map/all_to_all | solution.py:34
  363.5 323.8 %reduce-scatter.2.cloned.1.call-start = ((), (), s32[]{:S(2)}) async-start(), calls=%async_computation.12 | async-start | bytes 14155776 | tf_op jit(solution)/shard_map/reduce_scatter | solution.py:227
  375.9 8.0 %collective-permute-start.3 = (f32[2,3,512]{2,0,1:T(2,128)S(1)}, f32[2,3,512]{2,0,1:T(2,128)S(1)}, u32[]{:S(2)}, u32[]{:S(2)}) collective-permute-start(f32[2,3,512]{2,0,1:T(2,128)S(1)} %bitcast.216), channel_id=1, source_target_pairs={{0,1},{1,2},{2,3},{3,4},{4,5},{5,6},{6,7},{8,9},{9,10},{10,11},{11... | collective-permute-start | bytes 36872 | tf_op jit(solution)/shard_map/ppermute | solution.py:44
  396.3 11.8 %copy-start.28 = (f32[256,512]{1,0:T(8,128)}, f32[256,512]{1,0:T(8,128)S(1)}, u32[]{:S(2)}) copy-start(f32[256,512]{1,0:T(8,128)S(1)} %get-tuple-element.38) | copy-start | bytes 1572868
  396.4 6.3 collective-permute-start.5
  408.3 3.9 collective-permute-start.4
  418.6 6.0 collective-permute-start.6
  478.9 9.7 %collective-permute-start.7 = (bf16[256,512]{1,0:T(8,128)(2,1)S(1)}, bf16[256,512]{1,0:T(8,128)(2,1)S(1)}, u32[]{:S(2)}, u32[]{:S(2)}) collective-permute-start(bf16[256,512]{1,0:T(8,128)(2,1)S(1)} %fusion.37), channel_id=1, source_target_pairs={{64,0},{65,1},{66,2},{67,3},{68,4},{69,5},{70,6},{71,7},{72,8},{73... | collective-permute-start | bytes 786440 | tf_op jit(solution)/shard_map/ppermute | solution.py:44
  488.8 30.2 %copy-start.25 = (f32[1,256,512]{2,0,1:T(1,128)S(1)}, f32[1,256,512]{2,0,1:T(1,128)}, u32[]{:S(2)}) copy-start(f32[1,256,512]{2,0,1:T(1,128)} %copy-done.24) | copy-start | bytes 1572868
  524.9 6.6 collective-permute-start.8
  542.1 5.8 collective-permute-start.9
  585.1 9.5 %all-to-all-start.10 = ((bf16[8,3,3,512]{3,2,1,0:T(4,128)(2,1)}), bf16[8,3,3,512]{3,2,1,0:T(4,128)(2,1)S(1)}, u32[]{:S(2)}, u32[]{:S(2)}) async-start(bf16[8,3,3,512]{3,2,1,0:T(4,128)(2,1)} %broadcast_in_dim.84), calls=%async_computation.11 | async-start | bytes 196608 | tf_op jit(solution)/shard_map/all_to_all | solution.py:34
  595.7 25.4 %all-to-all-start.9 = ((bf16[8,128,512]{2,1,0:T(8,128)(2,1)}), bf16[8,128,512]{2,1,0:T(8,128)(2,1)S(1)}, u32[]{:S(2)}, u32[]{:S(2)}) async-start(bf16[8,128,512]{2,1,0:T(8,128)(2,1)} %broadcast_in_dim.83), calls=%async_computation.10 | async-start | bytes 2097152 | tf_op jit(solution)/shard_map/all_to_all | solution.py:34
  621.1 62.3 %all-to-all-start.8 = ((bf16[8,512,512]{2,1,0:T(8,128)(2,1)}), bf16[8,512,512]{2,1,0:T(8,128)(2,1)}, u32[]{:S(2)}, u32[]{:S(2)}) async-start(bf16[8,512,512]{2,1,0:T(8,128)(2,1)} %bitcast.179), calls=%async_computation.9 | async-start | bytes 8388608 | tf_op jit(solution)/shard_map/all_to_all | solution.py:55
  683.4 7.4 %copy-start.1 = (bf16[512,512]{1,0:T(8,128)(2,1)S(1)}, bf16[512,512]{1,0:T(8,128)(2,1)}, u32[]{:S(2)}) copy-start(bf16[512,512]{1,0:T(8,128)(2,1)} %param.9) | copy-start | bytes 1572868
  (39 other events, 125.8 us)
Sparse Core Ops, SparseCore 0:
  559.1 95.8 reduce-scatter.1
